TPU v7x, 32 devices: a whole 2x2x4 slice. The times are simulated.
32 devices in a mesh: lat: 4 (over y, x), kpt: 8 (over z, core).
Axes of the slice: x: 2, y: 2, z: 4, core: 2. Of those that a mesh axis runs over, the one named last changes fastest.
Arguments:
- coarse: bfloat16 [2, 4, 32, 12288], P(None, 'lat', 'kpt'), may hold values from -1 to 1
- rp_vectors: int32 [4, 3], P('lat'), may hold values from -4 to 4
- rp_weights: int32 [4], P('lat'), may hold values from 1 to 3
- re_vectors: int32 [32, 3], replicated, may hold values from -4 to 4
- re_weights: int32 [32], replicated, may hold values from 1 to 3
- q_points: float32 [2, 3], replicated, may hold values from 0 to 1
- k_points: float32 [512, 3], P('kpt'), may hold values from 0 to 1
- modes_rot: bfloat16 [2, 2, 48, 48], replicated, may hold values from -0.625 to 0.625
- u_k: bfloat16 [2, 512, 16, 16], P(None, 'kpt'), may hold values from -1 to 1
- u_kq: bfloat16 [2, 2, 512, 16, 16], P(None, None, 'kpt'), may hold values from -1 to 1
- mask_k: int32 [512, 16], P('kpt'), may hold values 0 or 1
- mask_kq: int32 [2, 512, 16], P(None, 'kpt'), may hold values 0 or 1
Outputs:
- coupling: bfloat16 [2, 512, 2, 12288], P(None, 'kpt', None, 'lat')
All inputs are finite; a program needn't handle non-finite values. No bound on the sum of `mask_k` or of `mask_kq` on one device may be relied on, other than what follows from the above.
Results may differ from a plain program's by a relative error of at most 0.017.
Values may be sent and summed in bfloat16 or wider, within the bound.
A program may use at most 128 MiB of HBM per device.

v0:
```python
import jax
import jax.numpy as jnp
from jax import lax
from jax.sharding import PartitionSpec as P

two_pi = 6.283185307179586


def phases(points, vectors, weights):
    cells = vectors.astype(jnp.float32)
    argument = two_pi * (
        points[:, 0:1] * cells[None, :, 0]
        + points[:, 1:2] * cells[None, :, 1]
        + points[:, 2:3] * cells[None, :, 2]
    )
    inverse = 1.0 / weights.astype(jnp.float32)
    return (
        (jnp.cos(argument) * inverse).astype(jnp.bfloat16),
        (jnp.sin(argument) * inverse).astype(jnp.bfloat16),
    )


def rotate_modes(values, modes_rot):
    shape = values.shape
    mode_count = modes_rot.shape[2]
    split = values.reshape(shape[0], shape[1], shape[2], mode_count, shape[3] // mode_count)
    br = jnp.einsum(
        "qmn,qrmx->qrnx", modes_rot[0], split[0], preferred_element_type=jnp.float32
    ) - jnp.einsum("qmn,qrmx->qrnx", modes_rot[1], split[1], preferred_element_type=jnp.float32)
    bi = jnp.einsum(
        "qmn,qrmx->qrnx", modes_rot[0], split[1], preferred_element_type=jnp.float32
    ) + jnp.einsum("qmn,qrmx->qrnx", modes_rot[1], split[0], preferred_element_type=jnp.float32)
    return jnp.stack([br, bi]).reshape(shape).astype(jnp.bfloat16)


def phonon_sum(block, vectors, weights, q_points):
    phase_real, phase_imag = phases(q_points, vectors, weights)
    rows = block.shape[1]
    cells = block.shape[2]
    lanes = block.shape[3]
    flat_real = block[0].reshape(rows, cells * lanes)
    flat_imag = block[1].reshape(rows, cells * lanes)
    part_real = jnp.dot(phase_real, flat_real, preferred_element_type=jnp.float32) - jnp.dot(
        phase_imag, flat_imag, preferred_element_type=jnp.float32
    )
    part_imag = jnp.dot(phase_real, flat_imag, preferred_element_type=jnp.float32) + jnp.dot(
        phase_imag, flat_real, preferred_element_type=jnp.float32
    )
    return jnp.stack([part_real, part_imag]).reshape(2, q_points.shape[0], cells, lanes)


def per_device(
    coarse,
    rp_vectors,
    rp_weights,
    re_vectors,
    re_weights,
    q_points,
    k_points,
    modes_rot,
    u_k,
    u_kq,
    mask_k,
    mask_kq,
):
    q_count = q_points.shape[0]
    k_count = k_points.shape[0]
    band_count = u_k.shape[2]
    all_vectors, all_weights = (
        lax.all_gather(rp_vectors, "lat", axis=0, tiled=True),
        lax.all_gather(rp_weights, "lat", axis=0, tiled=True),
    )
    blocks = lax.all_to_all(coarse, "lat", split_axis=2, concat_axis=1, tiled=True)
    summed = phonon_sum(blocks, all_vectors, all_weights, q_points).astype(jnp.bfloat16)
    rotated = rotate_modes(summed, modes_rot)
    shared = lax.all_to_all(rotated, "lat", split_axis=3, concat_axis=2, tiled=True)
    lane_local = shared.shape[3]
    portion = lax.all_gather(shared, "kpt", axis=2, tiled=True)
    kreal, kimag = phases(k_points, re_vectors, re_weights)
    er = jnp.einsum(
        "kr,qrx->kqx", kreal, portion[0], preferred_element_type=jnp.float32
    ) - jnp.einsum("kr,qrx->kqx", kimag, portion[1], preferred_element_type=jnp.float32)
    ei = jnp.einsum(
        "kr,qrx->kqx", kreal, portion[1], preferred_element_type=jnp.float32
    ) + jnp.einsum("kr,qrx->kqx", kimag, portion[0], preferred_element_type=jnp.float32)
    totals = jnp.stack([er, ei])
    mode_local = lane_local // (band_count * band_count)
    field = totals.astype(jnp.bfloat16).reshape(
        2, k_count, q_count, mode_local, band_count, band_count
    )
    tr = jnp.einsum(
        "kqmab,kbn->kqman", field[0], u_k[0], preferred_element_type=jnp.float32
    ) - jnp.einsum("kqmab,kbn->kqman", field[1], u_k[1], preferred_element_type=jnp.float32)
    ti = jnp.einsum(
        "kqmab,kbn->kqman", field[0], u_k[1], preferred_element_type=jnp.float32
    ) + jnp.einsum("kqmab,kbn->kqman", field[1], u_k[0], preferred_element_type=jnp.float32)
    tr = tr.astype(jnp.bfloat16)
    ti = ti.astype(jnp.bfloat16)
    outr = jnp.einsum(
        "qkac,kqman->kqmcn", u_kq[0], tr, preferred_element_type=jnp.float32
    ) + jnp.einsum("qkac,kqman->kqmcn", u_kq[1], ti, preferred_element_type=jnp.float32)
    outi = jnp.einsum(
        "qkac,kqman->kqmcn", u_kq[0], ti, preferred_element_type=jnp.float32
    ) - jnp.einsum("qkac,kqman->kqmcn", u_kq[1], tr, preferred_element_type=jnp.float32)
    window = (
        jnp.transpose(mask_kq.astype(jnp.float32), (1, 0, 2))[:, :, None, :, None]
        * mask_k.astype(jnp.float32)[:, None, None, None, :]
    )
    result = jnp.stack([outr * window, outi * window])
    return result.reshape(2, k_count, q_count, lane_local).astype(jnp.bfloat16)


def solution(mesh):
    placed = (
        P(None, "lat", "kpt", None),
        P("lat", None),
        P("lat"),
        P(),
        P(),
        P(),
        P("kpt", None),
        P(),
        P(None, "kpt", None, None),
        P(None, None, "kpt", None, None),
        P("kpt", None),
        P(None, "kpt", None),
    )
    return jax.shard_map(
        per_device,
        mesh=mesh,
        in_specs=placed,
        out_specs=P(None, "kpt", None, "lat"),
        check_vma=False,
    )
```

profile of v0, /device:TPU:0, one launch (start us, length us, event | category | flops | bytes accessed | tf_op | source)
XLA Modules:
  0.0 252.8 jit_solution(12334398810767427954)
XLA Ops:
  4.4 5.2 %all-to-all-start = ((bf16[2,1,4,12288]{3,0,1,2:T(2,128)(2,1)}), bf16[2,1,4,12288]{3,0,1,2:T(2,128)(2,1)S(1)}, u32[]{:S(2)}, u32[]{:S(2)}) async-start(bf16[2,1,4,12288]{3,0,1,2:T(2,128)(2,1)} %copy.132), calls=%async_computation | async-start | bytes 393216 | tf_op jit(solution)/shard_map/all_to_all | solution.py:73
  9.6 7.9 %all-reduce = s32[4]{0:T(128)S(1)} all-reduce(s32[4]{0:T(128)S(1)} %dynamic-update-slice), channel_id=1, replica_groups=mesh['lat'=4,'kpt'=8] {'lat'}, use_global_device_ids=true, to_apply=%add | all-reduce | flops 4 | bytes 32
  19.3 7.8 %all-gather = s32[4,1,3]{2,1,0:T(1,128)S(1)} all-gather(s32[1,1,3]{2,1,0:T(1,128)} %bitcast.155), channel_id=1, replica_groups=mesh['lat'=4,'kpt'=8] {'lat'}, dimensions={0}, use_global_device_ids=true | all-gather | bytes 60 | tf_op jit(solution)/shard_map/all_gather | solution.py:70
  37.3 10.0 %copy.135 = bf16[2,2,1,12288]{1,0,2,3:T(2,128)(2,1)} copy(bf16[2,2,1,12288]{3,1,2,0:T(2,128)(2,1)S(1)} %pad_maximum_fusion.1) | data formatting | bytes 196608 | tf_op jit(solution)/shard_map/stack | solution.py:33
  47.3 11.9 %reshape.167 = bf16[4,2,6144]{2,1,0:T(2,128)(2,1)} reshape(bf16[12288,1,2,2]{3,2,1,0:T(2,128)(2,1)} %bitcast.144) | data formatting | bytes 196608
  67.5 14.7 %reshape.168 = bf16[12288,1,2,2]{3,2,1,0:T(2,128)(2,1)} reshape(bf16[4,2,6144]{2,1,0:T(2,128)(2,1)S(1)} %all-to-all-done.1) | data formatting | bytes 196608
  82.2 12.7 %copy.137 = bf16[2,2,4,3072]{3,1,0,2:T(2,128)(2,1)S(1)} copy(bf16[2,2,4,3072]{1,0,3,2:T(2,128)(2,1)} %bitcast.145) | data formatting | bytes 196608 | tf_op jit(solution)/shard_map/all_to_all | solution.py:76
  94.8 16.5 %all_gather.11 = bf16[2,2,32,3072]{3,1,0,2:T(2,128)(2,1)S(1)} all-gather(bf16[2,2,4,3072]{3,1,0,2:T(2,128)(2,1)S(1)} %copy.137), channel_id=1, replica_groups=mesh['lat'=4,'kpt'=8] {'kpt'}, dimensions={2}, use_global_device_ids=true | all-gather | bytes 884736 | tf_op jit(solution)/shard_map/all_gather | solution.py:78
  120.0 9.8 %copy.142 = bf16[64,2,12,16,16]{4,3,2,1,0:T(8,128)(2,1)} copy(bf16[64,2,12,16,16]{0,4,3,2,1:T(8,128)(2,1)S(1)} %bitcast.147) | data formatting | bytes 1572864 | tf_op jit(solution)/shard_map/squeeze | solution.py:92
  129.8 10.8 %copy.145 = bf16[64,2,12,16,16]{4,3,2,1,0:T(8,128)(2,1)} copy(bf16[64,2,12,16,16]{0,4,3,2,1:T(8,128)(2,1)} %bitcast.146) | data formatting | bytes 1572864 | tf_op jit(solution)/shard_map/squeeze | solution.py:93
  140.6 9.2 %fusion.23 = f32[64,2,12,16,16]{4,3,2,1,0:T(8,128)} fusion(bf16[64,2,12,16,16]{4,3,2,1,0:T(8,128)(2,1)} %copy.142, bf16[1,64,16,16]{3,2,1,0:T(8,128)(2,1)} %copy.176), kind=kOutput, calls=%fused_computation.36 | convolution fusion | flops 12582912 | bytes 2392064 | tf_op jit(solution)/shard_map/kqmab,kbn->kqman/dot_general | solution.py:94
  149.8 5.5 %fusion.21 = f32[64,2,12,16,16]{4,3,2,1,0:T(8,128)} fusion(bf16[64,2,12,16,16]{4,3,2,1,0:T(8,128)(2,1)S(1)} %bitcast.143, bf16[1,64,16,16]{3,2,1,0:T(8,128)(2,1)S(1)} %copy.175), kind=kOutput, calls=%fused_computation.34 | convolution fusion | flops 12582912 | bytes 2392064 | tf_op jit(solution)/shard_map/kqmab,kbn->kqman/dot_general | solution.py:91
  155.3 8.2 %add_convert_fusion = bf16[64,2,12,16,16]{4,3,2,1,0:T(8,128)(2,1)S(1)} fusion(f32[64,2,12,16,16]{4,3,2,1,0:T(8,128)} %fusion.23, bf16[64,2,12,16,16]{4,3,2,1,0:T(8,128)(2,1)} %copy.145, bf16[1,64,16,16]{3,2,1,0:T(8,128)(2,1)S(1)} %copy.175), kind=kOutput, calls=%fused_computation.4 | convolution fusion | flops 13369344 | bytes 3178496 | tf_op jit(solution)/shard_map/kqmab,kbn->kqman/dot_general | solution.py:96
  163.5 10.9 %subtract_convert_fusion = bf16[64,2,12,16,16]{4,3,2,1,0:T(8,128)(2,1)} fusion(f32[64,2,12,16,16]{4,3,2,1,0:T(8,128)} %fusion.21, bf16[64,2,12,16,16]{4,3,2,1,0:T(8,128)(2,1)} %copy.145, bf16[1,64,16,16]{3,2,1,0:T(8,128)(2,1)S(1)} %copy-done.1), kind=kOutput, calls=%fused_computation.5 | convolution fusion | flops 13369344 | bytes 3178496 | tf_op jit(solution)/shard_map/kqmab,kbn->kqman/dot_general | solution.py:93
  174.4 9.7 %fusion.10 = f32[64,2,12,16,16]{4,3,2,1,0:T(8,128)} fusion(bf16[64,2,12,16,16]{4,3,2,1,0:T(8,128)(2,1)} %subtract_convert_fusion, bf16[1,2,64,16,16]{4,3,1,2,0:T(8,128)(2,1)S(1)} %copy.178), kind=kOutput, calls=%fused_computation.21 | convolution fusion | flops 12582912 | bytes 2424832 | tf_op jit(solution)/shard_map/qkac,kqman->kqmcn/dot_general | solution.py:104
  184.1 5.7 %fusion.16 = f32[64,2,12,16,16]{4,3,2,1,0:T(8,128)} fusion(bf16[64,2,12,16,16]{4,3,2,1,0:T(8,128)(2,1)S(1)} %copy-done, bf16[1,2,64,16,16]{4,3,1,2,0:T(8,128)(2,1)S(1)} %copy.177), kind=kOutput, calls=%fused_computation.27 | convolution fusion | flops 12582912 | bytes 2424832 | tf_op jit(solution)/shard_map/qkac,kqman->kqmcn/dot_general | solution.py:99
  189.8 5.6 %fusion.14 = f32[64,2,12,16,16]{4,3,2,1,0:T(8,128)} fusion(bf16[64,2,12,16,16]{4,3,2,1,0:T(8,128)(2,1)S(1)} %add_convert_fusion, bf16[1,2,64,16,16]{4,3,1,2,0:T(8,128)(2,1)S(1)} %copy.177), kind=kOutput, calls=%fused_computation.25 | convolution fusion | flops 12582912 | bytes 2424832 | tf_op jit(solution)/shard_map/qkac,kqman->kqmcn/dot_general | solution.py:102
  195.5 5.8 %fusion.12 = f32[64,2,12,16,16]{4,3,2,1,0:T(8,128)} fusion(bf16[64,2,12,16,16]{4,3,2,1,0:T(8,128)(2,1)S(1)} %add_convert_fusion, bf16[1,2,64,16,16]{4,3,1,2,0:T(8,128)(2,1)S(1)} %copy.178), kind=kOutput, calls=%fused_computation.23 | convolution fusion | flops 12582912 | bytes 2424832 | tf_op jit(solution)/shard_map/qkac,kqman->kqmcn/dot_general | solution.py:101
  201.3 9.7 %copy.157 = f32[64,2,12,16,16]{0,3,4,2,1:T(8,128)S(1)} copy(f32[64,2,12,16,16]{4,3,2,1,0:T(8,128)} %fusion.10) | data formatting | bytes 3145728 | tf_op jit(solution)/shard_map/qkac,kqman->kqmcn/dot_general | solution.py:104
  211.0 10.9 %copy.152 = f32[64,2,12,16,16]{0,3,4,2,1:T(8,128)} copy(f32[64,2,12,16,16]{4,3,2,1,0:T(8,128)} %fusion.16) | data formatting | bytes 3145728 | tf_op jit(solution)/shard_map/qkac,kqman->kqmcn/dot_general | solution.py:99
  221.9 10.9 %copy.156 = f32[64,2,12,16,16]{0,3,4,2,1:T(8,128)} copy(f32[64,2,12,16,16]{4,3,2,1,0:T(8,128)} %fusion.14) | data formatting | bytes 3145728 | tf_op jit(solution)/shard_map/qkac,kqman->kqmcn/dot_general | solution.py:102
  232.8 10.9 %copy.153 = f32[64,2,12,16,16]{0,3,4,2,1:T(8,128)} copy(f32[64,2,12,16,16]{4,3,2,1,0:T(8,128)} %fusion.12) | data formatting | bytes 3145728 | tf_op jit(solution)/shard_map/qkac,kqman->kqmcn/dot_general | solution.py:101
  243.7 5.0 %fusion.5 = (bf16[64,2,12,16,16]{0,4,3,2,1:T(8,128)(2,1)S(1)}, bf16[64,2,12,16,16]{0,4,3,2,1:T(8,128)(2,1)S(1)}) fusion(f32[64,2,12,16,16]{0,3,4,2,1:T(8,128)} %copy.152, f32[64,2,12,16,16]{0,3,4,2,1:T(8,128)} %copy.153, f32[64,2,16,16]{0,3,2,1:T(8,128)S(1)} %copy-done.2, f32[64,2,12,16,16]{0,3,4,2,1:T(8,128)} %copy.156, f32[64,2,12,16,16]{0,3,4,2,1:T(8,128)S(1)} %copy.157), kind=kLoop, calls=%fused_computation.14 | loop fusion | flops 2359296 | bytes 7995392 | tf_op jit(solution)/shard_map/convert.3
  249.5 3.3 %copy.158 = bf16[2,64,2,3072]{3,2,1,0:T(2,128)(2,1)} copy(bf16[2,64,2,3072]{1,3,2,0:T(8,128)(2,1)S(1)} %pad_maximum_fusion) | data formatting | bytes 3145728 | tf_op jit(solution)/shard_map/stack | solution.py:109
  (58 shorter events, 33.2 us)
Async XLA Ops:
  4.4 27.8 %all-to-all-start = ((bf16[2,1,4,12288]{3,0,1,2:T(2,128)(2,1)}), bf16[2,1,4,12288]{3,0,1,2:T(2,128)(2,1)S(1)}, u32[]{:S(2)}, u32[]{:S(2)}) async-start(bf16[2,1,4,12288]{3,0,1,2:T(2,128)(2,1)} %copy.132), calls=%async_computation | async-start | bytes 393216 | tf_op jit(solution)/shard_map/all_to_all | solution.py:73
  37.3 25.3 %copy-start.3 = (s32[32]{0:T(128)S(1)}, s32[32]{0:T(128)}, u32[]{:S(2)}) copy-start(s32[32]{0:T(128)} %param.16) | copy-start | bytes 388
  59.3 8.2 %all-to-all-start.1 = ((bf16[4,2,6144]{2,1,0:T(2,128)(2,1)}), bf16[4,2,6144]{2,1,0:T(2,128)(2,1)S(1)}, u32[]{:S(2)}, u32[]{:S(2)}) async-start(bf16[4,2,6144]{2,1,0:T(2,128)(2,1)} %reshape.167), calls=%async_computation.1 | async-start | bytes 196608 | tf_op jit(solution)/shard_map/all_to_all | solution.py:76
  129.8 20.0 %slice-start = ((s8[6291456]{0:T(1024)(128)(4,1)}), s8[2097152]{0:T(1024)(128)(4,1)S(1)}, s32[]{:S(2)}) async-start(s8[6291456]{0:T(1024)(128)(4,1)} %bitcast.142), calls=%async_computation.2 | async-start | bytes 4194304
  140.6 9.2 %slice-start.1 = ((s8[6291456]{0:T(1024)(128)(4,1)}), s8[4194304]{0:T(1024)(128)(4,1)S(1)}, s32[]{:S(2)}) async-start(s8[6291456]{0:T(1024)(128)(4,1)} %bitcast.142), calls=%async_computation.3 | async-start | bytes 8388608
  155.3 8.2 %copy-start.1 = (bf16[1,64,16,16]{3,2,1,0:T(8,128)(2,1)S(1)}, bf16[1,64,16,16]{3,2,1,0:T(8,128)(2,1)}, u32[]{:S(2)}) copy-start(bf16[1,64,16,16]{3,2,1,0:T(8,128)(2,1)} %copy.176) | copy-start | bytes 98308
  174.4 9.7 %copy-start = (bf16[64,2,12,16,16]{4,3,2,1,0:T(8,128)(2,1)S(1)}, bf16[64,2,12,16,16]{4,3,2,1,0:T(8,128)(2,1)}, u32[]{:S(2)}) copy-start(bf16[64,2,12,16,16]{4,3,2,1,0:T(8,128)(2,1)} %subtract_convert_fusion) | copy-start | bytes 2359300
  232.8 10.9 %copy-start.2 = (f32[64,2,16,16]{0,3,2,1:T(8,128)S(1)}, f32[64,2,16,16]{0,3,2,1:T(8,128)}, u32[]{:S(2)}) copy-start(f32[64,2,16,16]{0,3,2,1:T(8,128)} %broadcast_multiply_fusion) | copy-start | bytes 393220
where the time goes:
time: 254 us; the launch traced here: 253 us
  local copies, waits for them, and re-layouts  131 us (52%)
  matrix products  69.2 us (27%)
  blocking collectives  32.2 us (13%)
  other arithmetic  8.81 us (3%)
  starting transfers between devices  8.5 us (3%)
    unnamed x22, local copies, waits for them, and re-layouts  33.1 us
    all_gather x1, blocking collectives, per_device(): portion = lax.all_gather(shared, 'kpt', axis=2, tiled=True)  16.5 us
    all_to_all x1, local copies, waits for them, and re-layouts, per_device(): lax.all_to_all(rotated, 'lat', split_axis=3, concat_axis=2, tiled=True)  12.7 us
    dot_general x1, local copies, waits for them, and re-layouts, per_device(): jnp.einsum('qkac,kqman->kqmcn', u_kq[1], ti, preferred_element_type=jnp.f...  10.9 us
    dot_general x1, local copies, waits for them, and re-layouts, per_device(): jnp.einsum('qkac,kqman->kqmcn', u_kq[0], tr, preferred_element_type=jnp.f...  10.9 us
    dot_general x1, local copies, waits for them, and re-layouts, per_device(): jnp.einsum('qkac,kqman->kqmcn', u_kq[0], ti, preferred_element_type=jnp.f...  10.9 us
    dot_general x1, matrix products, per_device(): jnp.einsum('kqmab,kbn->kqman', field[1], u_k[1], preferred_element_type=j...  10.9 us
    squeeze x1, local copies, waits for them, and re-layouts, per_device(): field[1]  10.8 us
  transfers between devices with their start and end apart: 2, of which 1 were waited for; matrix products, arithmetic and copies ran while one was open for 4% of the time, Pallas kernels for 0%

commit v1 on v0

--- a/solution.py
+++ b/solution.py
@@ -73,7 +73,10 @@
     blocks = lax.all_to_all(coarse, "lat", split_axis=2, concat_axis=1, tiled=True)
     summed = phonon_sum(blocks, all_vectors, all_weights, q_points).astype(jnp.bfloat16)
     rotated = rotate_modes(summed, modes_rot)
-    shared = lax.all_to_all(rotated, "lat", split_axis=3, concat_axis=2, tiled=True)
+    shared = jnp.concatenate(
+        lax.all_to_all(jnp.stack(jnp.split(rotated, lax.axis_size("lat"), axis=3)), "lat", 0, 0),
+        axis=2,
+    )
     lane_local = shared.shape[3]
     portion = lax.all_gather(shared, "kpt", axis=2, tiled=True)
     kreal, kimag = phases(k_points, re_vectors, re_weights)

time: 254 us -> 206 us (0.81)
  local copies, waits for them, and re-layouts: 131 us -> 81.7 us
    unnamed x22 -> x18, local copies, waits for them, and re-layouts: 33.1 us -> 6.49 us
    all_to_all x1 -> x0, local copies, waits for them, and re-layouts: 12.7 us -> none  [per_device(): lax.all_to_all(rotated, 'lat', split_axis=3, concat_axis=2, tiled=True)]
    another operation x3 -> x2, local copies, waits for them, and re-layouts: 10 us -> 0.04 us  [rotate_modes(): return jnp.stack([br, bi]).reshape(shape).astype(jnp.bfloat16)]
    another operation x2 -> x3, other arithmetic: 5.19 us -> 5.95 us
  transfers between devices with their start and end apart: 2 -> 2, of which waited for: 1 -> 1; matrix products, arithmetic and copies ran while one was open for 4% -> 5% of each run, Pallas kernels for 0% -> 0%
where the time goes in v1:
time: 206 us; the launch traced here: 204 us
  local copies, waits for them, and re-layouts  81.7 us (40%)
  matrix products  69.2 us (34%)
  blocking collectives  32.2 us (16%)
  other arithmetic  10.2 us (5%)
  starting transfers between devices  8.5 us (4%)
    all_gather x1, blocking collectives, per_device(): portion = lax.all_gather(shared, 'kpt', axis=2, tiled=True)  16.5 us
    dot_general x1, local copies, waits for them, and re-layouts, per_device(): jnp.einsum('qkac,kqman->kqmcn', u_kq[1], ti, preferred_element_type=jnp.f...  10.9 us
    dot_general x1, local copies, waits for them, and re-layouts, per_device(): jnp.einsum('qkac,kqman->kqmcn', u_kq[0], tr, preferred_element_type=jnp.f...  10.9 us
    dot_general x1, local copies, waits for them, and re-layouts, per_device(): jnp.einsum('qkac,kqman->kqmcn', u_kq[0], ti, preferred_element_type=jnp.f...  10.9 us
    dot_general x1, matrix products, per_device(): jnp.einsum('kqmab,kbn->kqman', field[1], u_k[1], preferred_element_type=j...  10.9 us
    squeeze x1, local copies, waits for them, and re-layouts, per_device(): field[1]  10.8 us
    squeeze x1, local copies, waits for them, and re-layouts, per_device(): field[0]  9.81 us
    dot_general x1, matrix products, per_device(): jnp.einsum('qkac,kqman->kqmcn', u_kq[1], tr, preferred_element_type=jnp.f...  9.73 us
  transfers between devices with their start and end apart: 2, of which 1 were waited for; matrix products, arithmetic and copies ran while one was open for 5% of the time, Pallas kernels for 0%

profile of v1, /device:TPU:0, one launch (start us, length us, event | category | flops | bytes accessed | tf_op | source)
XLA Modules:
  0.0 204.2 jit_solution(2790608858082249442)
XLA Ops:
  0.7 1.8 copy.220
  4.4 5.2 %all-to-all-start = ((bf16[2,1,4,12288]{3,0,1,2:T(2,128)(2,1)}), bf16[2,1,4,12288]{3,0,1,2:T(2,128)(2,1)S(1)}, u32[]{:S(2)}, u32[]{:S(2)}) async-start(bf16[2,1,4,12288]{3,0,1,2:T(2,128)(2,1)} %copy.220), calls=%async_computation | async-start | bytes 393216 | tf_op jit(solution)/shard_map/all_to_all | solution.py:73
  9.6 7.9 %all-reduce = s32[4]{0:T(128)S(1)} all-reduce(s32[4]{0:T(128)S(1)} %dynamic-update-slice), channel_id=1, replica_groups=mesh['lat'=4,'kpt'=8] {'lat'}, use_global_device_ids=true, to_apply=%add | all-reduce | flops 4 | bytes 32
  19.3 7.8 %all-gather.1 = s32[4,1,3]{2,1,0:T(1,128)S(1)} all-gather(s32[1,1,3]{2,1,0:T(1,128)} %bitcast.166), channel_id=1, replica_groups=mesh['lat'=4,'kpt'=8] {'lat'}, dimensions={0}, use_global_device_ids=true | all-gather | bytes 60 | tf_op jit(solution)/shard_map/all_gather | solution.py:70
  38.1 3.3 %all-to-all-start.1 = ((bf16[4,2,2,1,3072]{4,2,3,1,0:T(2,128)(2,1)}), bf16[4,2,2,1,3072]{4,2,3,1,0:T(2,128)(2,1)S(1)}, u32[]{:S(2)}, u32[]{:S(2)}) async-start(bf16[4,2,2,1,3072]{4,2,3,1,0:T(2,128)(2,1)} %maximum_bitcast_fusion), calls=%async_computation.1 | async-start | bytes 196608 | tf_op jit(solution)/shard_map/all_to_all | solution.py:77
  46.3 16.5 %all-gather = bf16[2,2,32,1,3072]{4,1,3,0,2:T(2,128)(2,1)S(1)} all-gather(bf16[2,2,4,1,3072]{4,1,3,0,2:T(2,128)(2,1)S(1)} %bitcast.158), channel_id=2, replica_groups=mesh['lat'=4,'kpt'=8] {'kpt'}, dimensions={2}, use_global_device_ids=true | all-gather | bytes 884736 | tf_op jit(solution)/shard_map/all_gather | solution.py:81
  65.8 2.4 %copy.231 = bf16[64,2,3072]{0,2,1:T(8,128)(2,1)} copy(bf16[64,2,3072]{2,0,1:T(8,128)(2,1)} %fusion.3) | data formatting | bytes 1572864 | tf_op jit(solution)/shard_map/convert.6
  69.7 1.8 copy.228
  71.4 9.8 %copy.230 = bf16[64,2,12,16,16]{4,3,2,1,0:T(8,128)(2,1)} copy(bf16[64,2,12,16,16]{0,4,3,2,1:T(8,128)(2,1)S(1)} %bitcast.155) | data formatting | bytes 1572864 | tf_op jit(solution)/shard_map/squeeze | solution.py:95
  81.3 10.8 %copy.233 = bf16[64,2,12,16,16]{4,3,2,1,0:T(8,128)(2,1)} copy(bf16[64,2,12,16,16]{0,4,3,2,1:T(8,128)(2,1)} %bitcast.154) | data formatting | bytes 1572864 | tf_op jit(solution)/shard_map/squeeze | solution.py:96
  92.0 9.2 %fusion.23 = f32[64,2,12,16,16]{4,3,2,1,0:T(8,128)} fusion(bf16[64,2,12,16,16]{4,3,2,1,0:T(8,128)(2,1)} %copy.230, bf16[1,64,16,16]{3,2,1,0:T(8,128)(2,1)} %copy.262), kind=kOutput, calls=%fused_computation.36 | convolution fusion | flops 12582912 | bytes 2392064 | tf_op jit(solution)/shard_map/kqmab,kbn->kqman/dot_general | solution.py:97
  101.2 5.5 %fusion.21 = f32[64,2,12,16,16]{4,3,2,1,0:T(8,128)} fusion(bf16[64,2,12,16,16]{4,3,2,1,0:T(8,128)(2,1)S(1)} %bitcast.153, bf16[1,64,16,16]{3,2,1,0:T(8,128)(2,1)S(1)} %copy.261), kind=kOutput, calls=%fused_computation.34 | convolution fusion | flops 12582912 | bytes 2392064 | tf_op jit(solution)/shard_map/kqmab,kbn->kqman/dot_general | solution.py:94
  106.7 8.2 %add_convert_fusion = bf16[64,2,12,16,16]{4,3,2,1,0:T(8,128)(2,1)S(1)} fusion(f32[64,2,12,16,16]{4,3,2,1,0:T(8,128)} %fusion.23, bf16[64,2,12,16,16]{4,3,2,1,0:T(8,128)(2,1)} %copy.233, bf16[1,64,16,16]{3,2,1,0:T(8,128)(2,1)S(1)} %copy.261), kind=kOutput, calls=%fused_computation.4 | convolution fusion | flops 13369344 | bytes 3178496 | tf_op jit(solution)/shard_map/kqmab,kbn->kqman/dot_general | solution.py:99
  115.0 10.9 %subtract_convert_fusion = bf16[64,2,12,16,16]{4,3,2,1,0:T(8,128)(2,1)} fusion(f32[64,2,12,16,16]{4,3,2,1,0:T(8,128)} %fusion.21, bf16[64,2,12,16,16]{4,3,2,1,0:T(8,128)(2,1)} %copy.233, bf16[1,64,16,16]{3,2,1,0:T(8,128)(2,1)S(1)} %copy-done.1), kind=kOutput, calls=%fused_computation.5 | convolution fusion | flops 13369344 | bytes 3178496 | tf_op jit(solution)/shard_map/kqmab,kbn->kqman/dot_general | solution.py:96
  125.8 9.7 %fusion.10 = f32[64,2,12,16,16]{4,3,2,1,0:T(8,128)} fusion(bf16[64,2,12,16,16]{4,3,2,1,0:T(8,128)(2,1)} %subtract_convert_fusion, bf16[1,2,64,16,16]{4,3,1,2,0:T(8,128)(2,1)S(1)} %copy.264), kind=kOutput, calls=%fused_computation.21 | convolution fusion | flops 12582912 | bytes 2424832 | tf_op jit(solution)/shard_map/qkac,kqman->kqmcn/dot_general | solution.py:107
  135.6 5.7 %fusion.16 = f32[64,2,12,16,16]{4,3,2,1,0:T(8,128)} fusion(bf16[64,2,12,16,16]{4,3,2,1,0:T(8,128)(2,1)S(1)} %copy-done, bf16[1,2,64,16,16]{4,3,1,2,0:T(8,128)(2,1)S(1)} %copy.263), kind=kOutput, calls=%fused_computation.27 | convolution fusion | flops 12582912 | bytes 2424832 | tf_op jit(solution)/shard_map/qkac,kqman->kqmcn/dot_general | solution.py:102
  141.3 5.6 %fusion.14 = f32[64,2,12,16,16]{4,3,2,1,0:T(8,128)} fusion(bf16[64,2,12,16,16]{4,3,2,1,0:T(8,128)(2,1)S(1)} %add_convert_fusion, bf16[1,2,64,16,16]{4,3,1,2,0:T(8,128)(2,1)S(1)} %copy.263), kind=kOutput, calls=%fused_computation.25 | convolution fusion | flops 12582912 | bytes 2424832 | tf_op jit(solution)/shard_map/qkac,kqman->kqmcn/dot_general | solution.py:105
  146.9 5.8 %fusion.12 = f32[64,2,12,16,16]{4,3,2,1,0:T(8,128)} fusion(bf16[64,2,12,16,16]{4,3,2,1,0:T(8,128)(2,1)S(1)} %add_convert_fusion, bf16[1,2,64,16,16]{4,3,1,2,0:T(8,128)(2,1)S(1)} %copy.264), kind=kOutput, calls=%fused_computation.23 | convolution fusion | flops 12582912 | bytes 2424832 | tf_op jit(solution)/shard_map/qkac,kqman->kqmcn/dot_general | solution.py:104
  152.7 9.7 %copy.245 = f32[64,2,12,16,16]{0,3,4,2,1:T(8,128)S(1)} copy(f32[64,2,12,16,16]{4,3,2,1,0:T(8,128)} %fusion.10) | data formatting | bytes 3145728 | tf_op jit(solution)/shard_map/qkac,kqman->kqmcn/dot_general | solution.py:107
  162.4 10.9 %copy.240 = f32[64,2,12,16,16]{0,3,4,2,1:T(8,128)} copy(f32[64,2,12,16,16]{4,3,2,1,0:T(8,128)} %fusion.16) | data formatting | bytes 3145728 | tf_op jit(solution)/shard_map/qkac,kqman->kqmcn/dot_general | solution.py:102
  173.3 10.9 %copy.244 = f32[64,2,12,16,16]{0,3,4,2,1:T(8,128)} copy(f32[64,2,12,16,16]{4,3,2,1,0:T(8,128)} %fusion.14) | data formatting | bytes 3145728 | tf_op jit(solution)/shard_map/qkac,kqman->kqmcn/dot_general | solution.py:105
  184.2 10.9 %copy.241 = f32[64,2,12,16,16]{0,3,4,2,1:T(8,128)} copy(f32[64,2,12,16,16]{4,3,2,1,0:T(8,128)} %fusion.12) | data formatting | bytes 3145728 | tf_op jit(solution)/shard_map/qkac,kqman->kqmcn/dot_general | solution.py:104
  195.1 5.0 %fusion.5 = (bf16[64,2,12,16,16]{0,4,3,2,1:T(8,128)(2,1)S(1)}, bf16[64,2,12,16,16]{0,4,3,2,1:T(8,128)(2,1)S(1)}) fusion(f32[64,2,12,16,16]{0,3,4,2,1:T(8,128)} %copy.240, f32[64,2,12,16,16]{0,3,4,2,1:T(8,128)} %copy.241, f32[64,2,16,16]{0,3,2,1:T(8,128)S(1)} %copy-done.2, f32[64,2,12,16,16]{0,3,4,2,1:T(8,128)} %copy.244, f32[64,2,12,16,16]{0,3,4,2,1:T(8,128)S(1)} %copy.245), kind=kLoop, calls=%fused_computation.14 | loop fusion | flops 2359296 | bytes 7995392 | tf_op jit(solution)/shard_map/convert.3
  200.9 3.3 %copy.246 = bf16[2,64,2,3072]{3,2,1,0:T(2,128)(2,1)} copy(bf16[2,64,2,3072]{1,3,2,0:T(8,128)(2,1)S(1)} %pad_maximum_fusion) | data formatting | bytes 3145728 | tf_op jit(solution)/shard_map/stack | solution.py:112
  (53 shorter events, 24.6 us)
Async XLA Ops:
  4.4 27.8 %all-to-all-start = ((bf16[2,1,4,12288]{3,0,1,2:T(2,128)(2,1)}), bf16[2,1,4,12288]{3,0,1,2:T(2,128)(2,1)S(1)}, u32[]{:S(2)}, u32[]{:S(2)}) async-start(bf16[2,1,4,12288]{3,0,1,2:T(2,128)(2,1)} %copy.220), calls=%async_computation | async-start | bytes 393216 | tf_op jit(solution)/shard_map/all_to_all | solution.py:73
  38.1 8.2 %all-to-all-start.1 = ((bf16[4,2,2,1,3072]{4,2,3,1,0:T(2,128)(2,1)}), bf16[4,2,2,1,3072]{4,2,3,1,0:T(2,128)(2,1)S(1)}, u32[]{:S(2)}, u32[]{:S(2)}) async-start(bf16[4,2,2,1,3072]{4,2,3,1,0:T(2,128)(2,1)} %maximum_bitcast_fusion), calls=%async_computation.1 | async-start | bytes 196608 | tf_op jit(solution)/shard_map/all_to_all | solution.py:77
  81.3 20.0 %slice-start = ((s8[6291456]{0:T(1024)(128)(4,1)}), s8[2097152]{0:T(1024)(128)(4,1)S(1)}, s32[]{:S(2)}) async-start(s8[6291456]{0:T(1024)(128)(4,1)} %bitcast.152), calls=%async_computation.2 | async-start | bytes 4194304
  92.0 9.2 %slice-start.1 = ((s8[6291456]{0:T(1024)(128)(4,1)}), s8[4194304]{0:T(1024)(128)(4,1)S(1)}, s32[]{:S(2)}) async-start(s8[6291456]{0:T(1024)(128)(4,1)} %bitcast.152), calls=%async_computation.3 | async-start | bytes 8388608
  106.7 8.2 %copy-start.1 = (bf16[1,64,16,16]{3,2,1,0:T(8,128)(2,1)S(1)}, bf16[1,64,16,16]{3,2,1,0:T(8,128)(2,1)}, u32[]{:S(2)}) copy-start(bf16[1,64,16,16]{3,2,1,0:T(8,128)(2,1)} %copy.262) | copy-start | bytes 98308
  125.8 9.7 %copy-start = (bf16[64,2,12,16,16]{4,3,2,1,0:T(8,128)(2,1)S(1)}, bf16[64,2,12,16,16]{4,3,2,1,0:T(8,128)(2,1)}, u32[]{:S(2)}) copy-start(bf16[64,2,12,16,16]{4,3,2,1,0:T(8,128)(2,1)} %subtract_convert_fusion) | copy-start | bytes 2359300
  184.2 10.9 %copy-start.2 = (f32[64,2,16,16]{0,3,2,1:T(8,128)S(1)}, f32[64,2,16,16]{0,3,2,1:T(8,128)}, u32[]{:S(2)}) copy-start(f32[64,2,16,16]{0,3,2,1:T(8,128)} %broadcast_multiply_fusion) | copy-start | bytes 393220
